TPU v7x, 768 devices: a whole 4x8x12 slice. The times are simulated.
768 devices in a mesh: section: 24 (over z, x_lo), tower: 2 (over x_hi), lane: 16 (over y, core).
Axes of the slice: x: 4 (x_hi: 2, x_lo: 2; x = x_hi * 2 + x_lo), y: 8, z: 12, core: 2. Of those that a mesh axis runs over, the one named last changes fastest.
Arguments:
- in_flight: bfloat16 [24, 2, 256, 3072], P('section', 'tower', 'lane'), may hold values from -6 to 6
- fresh_batches: bfloat16 [16, 2, 256, 3072], P(None, 'tower', 'lane'), may hold values from -6 to 6
- offsets: int32 [16], P('lane'), may hold values from 0 to 15, as said below
- norm_gain: float32 [24, 2, 3072], P('section', 'tower'), may hold values from 0.5 to 3
- w_query: bfloat16 [24, 2, 3072, 2048], P('section', 'tower', None, 'lane'), may hold values from -0.109375 to 0.109375
- w_keyval: bfloat16 [24, 2, 2, 3072, 2048], P('section', 'tower', None, None, 'lane'), may hold values from -0.109375 to 0.109375
- w_out: bfloat16 [24, 2, 2048, 3072], P('section', 'tower', 'lane'), may hold values from -0.125 to 0.125
Outputs:
- states: bfloat16 [2, 24, 2, 256, 3072], P(None, 'section', 'tower', 'lane')
Inputs may be any that keep to these rules, and one draw needn't show every extreme that they name: offsets is a permutation of 0 to 15.
All inputs are finite; a program needn't handle non-finite values.
Results may differ from a plain program's by a relative error of at most 0.017.
Values may be sent and summed in bfloat16 or wider, within the bound.
A program may use at most 32 MiB of HBM per device.

v0:
```python
import jax
import jax.numpy as jnp
from jax import lax
from jax.sharding import PartitionSpec as P

HEAD_DIM = 128


epsilon = 1e-06


def from_partner(value, axis, distance):
    mask = 2**distance
    pairs = [(source, source ^ mask) for source in range(lax.axis_size(axis))]
    return lax.ppermute(value, axis, pairs)


def side_by_side(arrays, axis, dim, along):
    widths = [a.shape[along] for a in arrays]
    both = jnp.concatenate(arrays, axis=along)
    filled = lax.all_gather(both, axis, axis=dim, tiled=True)
    return tuple(jnp.split(filled, [sum(widths[:k]) for k in range(1, len(widths))], axis=along))


def shifted(value, axis, steps):
    count = lax.axis_size(axis)
    leading, last = (max(0, -steps), min(count, count - steps))
    return lax.ppermute(value, axis, [(source, source + steps) for source in range(leading, last)])


def one_tick(state, norm_w, wq_local, wkv_local, wo_local):
    tok_rows = state.shape[0]
    wide = state.astype(jnp.float32)
    normed = (
        wide * lax.rsqrt(jnp.mean(wide * wide, -1, keepdims=True) + epsilon) * norm_w[None, :]
    ).astype(jnp.bfloat16)
    partner = from_partner(normed, "tower", 0)
    own_all, partner_all = side_by_side((normed, partner), "lane", 0, 1)
    all_rows = own_all.shape[0]
    clips = all_rows // tok_rows
    head_cols = wq_local.shape[1]
    heads_here = head_cols // HEAD_DIM
    query = jnp.dot(own_all, wq_local, preferred_element_type=jnp.float32).astype(jnp.bfloat16)
    keyval = jnp.einsum(
        "rd,cdh->crh", partner_all, wkv_local, preferred_element_type=jnp.float32
    ).astype(jnp.bfloat16)
    shaped = (clips, tok_rows, heads_here, HEAD_DIM)
    scores = jnp.einsum(
        "lqhe,lkhe->lhqk",
        query.reshape(shaped),
        keyval[0].reshape(shaped),
        preferred_element_type=jnp.float32,
    ) / jnp.sqrt(jnp.float32(HEAD_DIM))
    attn_weights = jax.nn.softmax(scores, axis=-1).astype(jnp.bfloat16)
    mixed = jnp.einsum(
        "lhqk,lkhe->lqhe",
        attn_weights,
        keyval[1].reshape(shaped),
        preferred_element_type=jnp.float32,
    ).astype(jnp.bfloat16)
    mixed = mixed.reshape(all_rows, head_cols)
    head_total = lax.psum_scatter(
        jnp.dot(mixed, wo_local, preferred_element_type=jnp.float32),
        "lane",
        scatter_dimension=0,
        tiled=True,
    )
    return (wide + head_total).astype(jnp.bfloat16)


def shards(in_flight, fresh_batches, offsets, norm_gain, w_query, w_keyval, w_out):
    norm_w = norm_gain[0, 0]
    wq_local = w_query[0, 0]
    wkv_local = w_keyval[0, 0]
    wo_local = w_out[0, 0]
    first = one_tick(in_flight[0, 0], norm_w, wq_local, wkv_local, wo_local)
    handed = shifted(first, "section", 1)
    picked = lax.dynamic_index_in_dim(fresh_batches[:, 0], offsets[0], 0, keepdims=False)
    section_pos = lax.axis_index("section")
    second_in = jnp.where(section_pos == 0, picked, handed)
    second = one_tick(second_in, norm_w, wq_local, wkv_local, wo_local)
    return jnp.stack([first, second])[:, None, None]


def solution(mesh):
    placed = (
        P("section", "tower", "lane", None),
        P(None, "tower", "lane", None),
        P("lane"),
        P("section", "tower", None),
        P("section", "tower", None, "lane"),
        P("section", "tower", None, None, "lane"),
        P("section", "tower", "lane", None),
    )
    return jax.shard_map(
        shards,
        mesh=mesh,
        in_specs=placed,
        out_specs=P(None, "section", "tower", "lane", None),
        check_vma=False,
    )
```

profile of v0, /device:TPU:1, one launch (start us, length us, event | category | flops | bytes accessed | tf_op | source)
XLA Modules:
  0.0 284.3 jit_solution(4073167156854211275)
XLA Ops:
  6.5 0.0 copy-start
  6.5 0.0 all-gather.3.cloned.1.call-start
  6.5 1.1 fusion.42
  7.7 1.0 fusion.44
  8.7 5.5 %collective-permute-start = (bf16[16,3072]{1,0:T(8,128)(2,1)S(1)}, bf16[16,3072]{1,0:T(8,128)(2,1)S(1)}, u32[]{:S(2)}, u32[]{:S(2)}) collective-permute-start(bf16[16,3072]{1,0:T(8,128)(2,1)S(1)} %fusion.44), channel_id=1, source_target_pairs={{0,16},{16,0},{1,17},{17,1},{2,18},{18,2},{3,19},{19,3},{4,20},{20... | collective-permute-start | bytes 294920 | tf_op jit(solution)/shard_map/ppermute | solution.py:15
  14.2 2.0 collective-permute-done
  16.2 0.7 pad_maximum_fusion
  16.9 0.0 all-gather.3.cloned.1.call-update
  16.9 0.0 copy-start.6
  16.9 0.0 reduce-scatter.3.cloned.1.call-start
  16.9 54.3 %all-gather.3.cloned.1.call-done = bf16[256,6144]{1,0:T(8,128)(2,1)} async-done(((bf16[16,6144]{1,0:T(8,128)(2,1)}), bf16[256,6144]{1,0:T(8,128)(2,1)}) %all-gather.3.cloned.1.call-update) | async-done | bytes 3145744 | tf_op jit(solution)/shard_map/all_gather | solution.py:21
  71.2 0.0 copy-done
  71.2 0.0 copy-start.4
  71.2 2.1 fusion.21
  73.4 0.0 copy-done.6
  73.4 0.2 copy-done.4
  73.6 0.0 copy-start.1
  73.6 0.6 fusion.26
  74.1 0.2 fusion.55
  74.3 0.2 convolution_multiply_fusion.1
  74.5 0.2 convolution_convert_fusion.1
  74.7 0.0 copy-done.1
  74.7 2.2 fusion.34
  77.0 0.0 copy-start.2
  77.0 0.0 copy-start.3
  77.0 0.0 reduce-scatter.3.cloned.1.call-update
  77.0 0.0 all-gather.5.cloned.1.call-start
  77.1 64.3 %reduce-scatter.3.cloned.1.call-done = f32[16,3072]{1,0:T(8,128)} async-done(((f32[256,3072]{1,0:T(8,128)}), f32[16,3072]{1,0:T(8,128)}) %reduce-scatter.3.cloned.1.call-update) | async-done | bytes 196624 | tf_op jit(solution)/shard_map/reduce_scatter | solution.py:62
  141.4 0.0 copy-done.2
  141.4 0.9 fusion.45
  142.4 1.4 collective-permute-start.1
  144.4 1.0 collective-permute-done.1
  145.3 1.0 fusion.38
  146.4 0.0 copy-done.3
  146.4 0.1 fusion.40
  146.5 4.3 %collective-permute-start.2 = (bf16[16,3072]{1,0:T(8,128)(2,1)S(1)}, bf16[16,3072]{1,0:T(8,128)(2,1)S(1)}, u32[]{:S(2)}, u32[]{:S(2)}) collective-permute-start(bf16[16,3072]{1,0:T(8,128)(2,1)S(1)} %fusion.40), channel_id=1, source_target_pairs={{0,16},{16,0},{1,17},{17,1},{2,18},{18,2},{3,19},{19,3},{4,20},{20... | collective-permute-start | bytes 294920 | tf_op jit(solution)/shard_map/ppermute | solution.py:15
  150.8 2.5 collective-permute-done.2
  153.4 0.7 pad_maximum_fusion.1
  154.0 0.0 all-gather.5.cloned.1.call-update
  154.1 0.0 reduce-scatter.5.cloned.1.call-start
  154.1 51.8 %all-gather.5.cloned.1.call-done = bf16[256,6144]{1,0:T(8,128)(2,1)} async-done(((bf16[16,6144]{1,0:T(8,128)(2,1)}), bf16[256,6144]{1,0:T(8,128)(2,1)}) %all-gather.5.cloned.1.call-update) | async-done | bytes 3145744 | tf_op jit(solution)/shard_map/all_gather | solution.py:21
  206.0 0.0 copy-start.5
  206.0 2.1 fusion.18
  208.1 0.2 copy-done.5
  208.3 0.6 fusion.29
  208.9 0.2 fusion.56
  209.1 0.2 convolution_multiply_fusion
  209.3 0.2 convolution_convert_fusion
  209.5 2.2 fusion.32
  211.7 0.0 reduce-scatter.5.cloned.1.call-update
  211.7 64.4 %reduce-scatter.5.cloned.1.call-done = f32[16,3072]{1,0:T(8,128)} async-done(((f32[256,3072]{1,0:T(8,128)}), f32[16,3072]{1,0:T(8,128)}) %reduce-scatter.5.cloned.1.call-update) | async-done | bytes 196624 | tf_op jit(solution)/shard_map/reduce_scatter | solution.py:62
  276.1 0.9 fusion.46
  277.1 0.7 maximum_bitcast_fusion
  (4 shorter events, 0.0 us)
Async XLA Ops:
  6.5 64.7 %copy-start = (bf16[1,1,2,3072,128]{4,3,2,1,0:T(8,128)(2,1)S(1)}, bf16[1,1,2,3072,128]{4,3,2,1,0:T(8,128)(2,1)}, u32[]{:S(2)}) copy-start(bf16[1,1,2,3072,128]{4,3,2,1,0:T(8,128)(2,1)} %param.12) | copy-start | bytes 4718596
  6.5 64.7 %all-gather.3.cloned.1.call-start = ((), (), s32[]{:S(2)}) async-start(), calls=%async_computation.2 | async-start | bytes 3342336 | tf_op jit(solution)/shard_map/all_gather | solution.py:21
  8.7 7.5 %collective-permute-start = (bf16[16,3072]{1,0:T(8,128)(2,1)S(1)}, bf16[16,3072]{1,0:T(8,128)(2,1)S(1)}, u32[]{:S(2)}, u32[]{:S(2)}) collective-permute-start(bf16[16,3072]{1,0:T(8,128)(2,1)S(1)} %fusion.44), channel_id=1, source_target_pairs={{0,16},{16,0},{1,17},{17,1},{2,18},{18,2},{3,19},{19,3},{4,20},{20... | collective-permute-start | bytes 294920 | tf_op jit(solution)/shard_map/ppermute | solution.py:15
  16.9 56.5 %copy-start.6 = (bf16[1,1,3072,128]{3,2,1,0:T(8,128)(2,1)S(1)}, bf16[1,1,3072,128]{3,2,1,0:T(8,128)(2,1)}, u32[]{:S(2)}) copy-start(bf16[1,1,3072,128]{3,2,1,0:T(8,128)(2,1)} %param.11) | copy-start | bytes 2359300
  16.9 124.5 %reduce-scatter.3.cloned.1.call-start = ((), (), s32[]{:S(2)}) async-start(), calls=%async_computation.3 | async-start | bytes 3342336 | tf_op jit(solution)/shard_map/reduce_scatter | solution.py:62
  71.2 2.4 copy-start.4
  73.6 1.2 copy-start.1
  77.0 64.4 %copy-start.2 = (bf16[1,1,16,3072]{3,2,1,0:T(8,128)(2,1)S(1)}, bf16[1,1,16,3072]{3,2,1,0:T(8,128)(2,1)}, u32[]{:S(2)}) copy-start(bf16[1,1,16,3072]{3,2,1,0:T(8,128)(2,1)} %param.7) | copy-start | bytes 294916
  77.0 69.4 %copy-start.3 = (f32[1,1,3072]{2,1,0:T(1,128)S(1)}, f32[1,1,3072]{2,1,0:T(1,128)}, u32[]{:S(2)}) copy-start(f32[1,1,3072]{2,1,0:T(1,128)} %param.10) | copy-start | bytes 36868
  77.0 128.9 %all-gather.5.cloned.1.call-start = ((), (), s32[]{:S(2)}) async-start(), calls=%async_computation.4 | async-start | bytes 3342336 | tf_op jit(solution)/shard_map/all_gather | solution.py:21
  142.4 3.0 %collective-permute-start.1 = (bf16[16,3072]{1,0:T(8,128)(2,1)S(1)}, bf16[16,3072]{1,0:T(8,128)(2,1)S(1)}, u32[]{:S(2)}, u32[]{:S(2)}) collective-permute-start(bf16[16,3072]{1,0:T(8,128)(2,1)S(1)} %fusion.45), channel_id=1, source_target_pairs={{0,32},{32,64},{64,96},{96,128},{128,160},{160,192},{192,224},{224... | collective-permute-start | bytes 294920 | tf_op jit(solution)/shard_map/ppermute | solution.py:28
  146.5 6.9 %collective-permute-start.2 = (bf16[16,3072]{1,0:T(8,128)(2,1)S(1)}, bf16[16,3072]{1,0:T(8,128)(2,1)S(1)}, u32[]{:S(2)}, u32[]{:S(2)}) collective-permute-start(bf16[16,3072]{1,0:T(8,128)(2,1)S(1)} %fusion.40), channel_id=1, source_target_pairs={{0,16},{16,0},{1,17},{17,1},{2,18},{18,2},{3,19},{19,3},{4,20},{20... | collective-permute-start | bytes 294920 | tf_op jit(solution)/shard_map/ppermute | solution.py:15
  154.1 122.1 %reduce-scatter.5.cloned.1.call-start = ((), (), s32[]{:S(2)}) async-start(), calls=%async_computation.5 | async-start | bytes 3342336 | tf_op jit(solution)/shard_map/reduce_scatter | solution.py:62
  206.0 2.4 copy-start.5
Sparse Core Ops, SparseCore 0:
  17.0 54.1 all-gather.2
  77.1 64.2 reduce-scatter.2
  154.2 51.7 all-gather.4
  211.9 64.2 reduce-scatter.4
where the time goes:
time: 285 us; the launch traced here: 284 us
  waiting for transfers between devices  240 us (84%)
  between operations  13.9 us (5%)
  starting transfers between devices  11.3 us (4%)
  matrix products  11 us (4%)
  other arithmetic  7.25 us (3%)
    reduce_scatter x2, waiting for transfers between devices, one_tick(): lax.psum_scatter(jnp.dot(mixed, wo_local, preferred_element_type=jnp.floa...  129 us
    all_gather x2, waiting for transfers between devices, side_by_side(): filled = lax.all_gather(both, axis, axis=dim, tiled=True)  106 us
    ppermute x2, starting transfers between devices, from_partner(): return lax.ppermute(value, axis, pairs)  9.78 us
  transfers between devices with their start and end apart: 7, of which 7 were waited for; matrix products, arithmetic and copies ran while one was open for 0% of the time, Pallas kernels for 0%

commit v1 on v0

v1 whole, which is shorter than its diff:
```python
import functools
import math

import jax
import jax.numpy as jnp
from jax import lax
from jax.experimental import pallas as pl
from jax.experimental.pallas import tpu as pltpu
from jax.sharding import PartitionSpec as P

HEAD = 128
EPS = 1e-06
MESH = pl.DeviceIdType.MESH
BF = jnp.bfloat16
F32 = jnp.float32
STAGES = ((0, 1), (1, 3), (3, 5), (5, 7), (7, 8))
BACK = (0, 1, 3, 5, 7)
AHEAD = (0, 2, 4, 6, 7)


def normed(rows, gain):
    wide = rows.astype(F32)
    mean = jnp.mean(wide * wide, -1, keepdims=True)
    return (wide * lax.rsqrt(mean + EPS) * gain).astype(BF)


def kernel(
    n_sec,
    n_lane,
    x_ref,
    fresh_ref,
    off_ref,
    gain_ref,
    wq_ref,
    wkv_ref,
    wo_ref,
    out_ref,
    xo,
    xp,
    gains,
    w_all,
    wo_all,
    fresh,
    rows,
    part,
    rsend,
    rrecv,
    outv,
    ag_s,
    ag_r,
    rs_s,
    rs_r,
    in_s,
    in_r,
    w_s,
    w_r,
    load,
):
    section = lax.axis_index("section")
    tower = lax.axis_index("tower")
    lane = lax.axis_index("lane")
    d = x_ref.shape[-1]
    hd = d // 2
    tok = x_ref.shape[0]
    up = {"lane": lax.rem(lane + 2, n_lane)}
    down = {"lane": lax.rem(lane + n_lane - 2, n_lane)}
    mate = {"lane": lane + 1 - 2 * lax.rem(lane, 2)}
    other = {"tower": 1 - tower}
    later = lax.rem(section + 1, n_sec)
    sooner = lax.rem(section + n_sec - 1, n_sec)

    loads = [
        (x_ref, xo.at[0]),
        (gain_ref, gains.at[0]),
        (wq_ref, w_all.at[:, pl.ds(0, HEAD)]),
        (wkv_ref.at[0], w_all.at[:, pl.ds(2 * HEAD, HEAD)]),
        (wkv_ref.at[1], w_all.at[:, pl.ds(4 * HEAD, HEAD)]),
        (wo_ref, wo_all.at[pl.ds(0, HEAD)]),
    ]
    loads = [pltpu.make_async_copy(a, b, load.at[i]) for i, (a, b) in enumerate(loads)]
    for copy in loads:
        copy.start()

    barrier = pltpu.get_barrier_semaphore()
    near = [up, down, mate, other]
    near += [{"section": s, "tower": t} for s in (later, sooner) for t in (tower, 1 - tower)]
    for device in near:
        pl.semaphore_signal(barrier, inc=1, device_id=device, device_id_type=MESH)
    pl.semaphore_wait(barrier, len(near))

    def remote(src, dst, send, recv, device):
        return pltpu.make_async_remote_copy(
            src_ref=src, dst_ref=dst, send_sem=send, recv_sem=recv, device_id=device, device_id_type=MESH
        )

    swaps = [
        remote(x_ref, xp.at[0], in_s.at[2], in_r.at[2], other),
        remote(gain_ref, gains.at[1], in_s.at[3], in_r.at[3], other),
        remote(wq_ref, w_all.at[:, pl.ds(HEAD, HEAD)], w_s.at[0], w_r.at[0], mate),
        remote(wkv_ref.at[0], w_all.at[:, pl.ds(3 * HEAD, HEAD)], w_s.at[1], w_r.at[1], mate),
        remote(wkv_ref.at[1], w_all.at[:, pl.ds(5 * HEAD, HEAD)], w_s.at[2], w_r.at[2], mate),
        remote(wo_ref, wo_all.at[pl.ds(HEAD, HEAD)], w_s.at[3], w_r.at[3], mate),
    ]
    for copy in swaps:
        copy.start()

    first_section = section == 0
    pick = pltpu.make_async_copy(fresh_ref, fresh, load.at[6])

    @pl.when(first_section)
    def _():
        pick.start()

    started = list(swaps)

    def gather(t, which, half, src, dst, device):
        copy = remote(
            rows.at[t, which, half, src],
            rows.at[t, which, half, dst],
            ag_s.at[t, which, half, dst],
            ag_r.at[t, which, half, dst],
            device,
        )
        return copy

    def pass_on(t, which, half, stage):
        copies = []
        if stage < 3 or which == 0:
            copies.append(gather(t, which, half, BACK[stage], BACK[stage + 1], up))
        if stage < 3 or which == 1:
            copies.append(gather(t, which, half, AHEAD[stage], AHEAD[stage + 1], down))
        for copy in copies:
            copy.start()
        started.extend(copies)

    def arrive(t, which, half, slot):
        gather(t, which, half, slot, slot, up).wait_recv()

    def put_normed(t, which, raw):
        value = normed(raw, gains[which])
        for half in range(2):
            rows[t, which, half, 0] = value[:, half * hd : (half + 1) * hd]
            pass_on(t, which, half, 0)

    def project(t, which, stage, first, last):
        lo, hi = STAGES[stage]
        total = None
        for half in range(2):
            block = rows[t, which, half, lo:hi].reshape((hi - lo) * tok, hd)
            term = jnp.dot(block, w_all[half * hd : (half + 1) * hd, first:last], preferred_element_type=F32)
            total = term if total is None else total + term
        return total.astype(BF)

    def attend(stage, query, keyval):
        lo, hi = STAGES[stage]
        m = (hi - lo) * tok
        pieces = []
        for head in range(2):
            q = query[:, head * HEAD : (head + 1) * HEAD]
            k = keyval[:, head * HEAD : (head + 1) * HEAD]
            v = keyval[:, (2 + head) * HEAD : (3 + head) * HEAD]
            scores = lax.dot_general(q, k, (((1,), (1,)), ((), ())), preferred_element_type=F32) * (1 / math.sqrt(HEAD))
            if hi - lo > 1:
                mine = lax.broadcasted_iota(jnp.int32, (m, m), 0) // tok == lax.broadcasted_iota(jnp.int32, (m, m), 1) // tok
                scores = jnp.where(mine, scores, -jnp.inf)
            raised = jnp.exp(scores - jnp.max(scores, -1, keepdims=True))
            weights = (raised / jnp.sum(raised, -1, keepdims=True)).astype(BF)
            pieces.append(jnp.dot(weights, v, preferred_element_type=F32).astype(BF))
        mixed = jnp.concatenate(pieces, axis=1)
        for half in range(2):
            out = jnp.dot(mixed, wo_all[:, half * hd : (half + 1) * hd], preferred_element_type=F32)
            part[half, lo:hi] = out.reshape(hi - lo, tok, hd)

    def reduced(t, way, half, k):
        return remote(
            rsend.at[t, way, half, k - 1],
            rrecv.at[t, way, half, k - 1],
            rs_s.at[t, way, half, k - 1],
            rs_r.at[t, way, half, k - 1],
            down if way == 0 else up,
        )

    def reduce_step(t, way, half, k, opens):
        slot = (BACK if way == 0 else AHEAD)[k]
        value = part[half, slot]
        if not opens:
            reduced(t, way, half, k + 1).wait_recv()
            value = value + rrecv[t, way, half, k].astype(F32)
        rsend[t, way, half, k - 1] = value.astype(BF)
        copy = reduced(t, way, half, k)
        copy.start()
        started.append(copy)

    def reduce_pair(t, k, long):
        for way in range(2):
            half = way if long else 1 - way
            reduce_step(t, way, half, k, k == (4 if long else 3))

    for t in range(2):
        if t == 0:
            loads[0].wait()
            loads[1].wait()
        else:

            @pl.when(section > 0)
            def _():
                remote(outv.at[0], xo.at[1], in_s.at[0], in_r.at[0], up).wait_recv()

        put_normed(t, 0, xo[t])
        if t == 0:
            swaps[0].wait_recv()
            swaps[1].wait_recv()
        else:
            remote(outv.at[0], xp.at[1], in_s.at[1], in_r.at[1], up).wait_recv()
        put_normed(t, 1, xp[t])
        if t == 0:
            for copy in loads[2:]:
                copy.wait()
            for copy in swaps[2:]:
                copy.wait_recv()

            @pl.when(first_section)
            def _():
                pick.wait()
                xo[1] = fresh[off_ref[0]]
                remote(xo.at[1], xp.at[1], in_s.at[1], in_r.at[1], other).start()

        query = project(t, 0, 0, 0, 2 * HEAD)
        attend(0, query, project(t, 1, 0, 2 * HEAD, 6 * HEAD))
        for stage in range(1, 4):
            for half in range(2):
                arrive(t, 0, half, BACK[stage])
                arrive(t, 0, half, AHEAD[stage])
                pass_on(t, 0, half, stage)
            query = project(t, 0, stage, 0, 2 * HEAD)
            for half in range(2):
                arrive(t, 1, half, BACK[stage])
                arrive(t, 1, half, AHEAD[stage])
                pass_on(t, 1, half, stage)
            attend(stage, query, project(t, 1, stage, 2 * HEAD, 6 * HEAD))
        reduce_pair(t, 3, False)
        arrive(t, 0, 0, 7)
        arrive(t, 0, 1, 7)
        query = project(t, 0, 4, 0, 2 * HEAD)
        arrive(t, 1, 0, 7)
        arrive(t, 1, 1, 7)
        attend(4, query, project(t, 1, 4, 2 * HEAD, 6 * HEAD))
        reduce_pair(t, 4, True)
        reduce_pair(t, 2, False)
        reduce_pair(t, 3, True)
        reduce_pair(t, 1, False)
        reduce_pair(t, 2, True)
        reduce_pair(t, 1, True)
        for half in range(2):
            total = part[half, 0]
            for way in range(2):
                reduced(t, way, half, 1).wait_recv()
                total = total + rrecv[t, way, half, 0].astype(F32)
            cols = slice(half * hd, (half + 1) * hd)
            outv[t, :, cols] = (xo[t, :, cols].astype(F32) + total).astype(BF)
        if t == 0:

            @pl.when(section < n_sec - 1)
            def _():
                remote(outv.at[0], xo.at[1], in_s.at[0], in_r.at[0], {"section": later, "tower": tower}).start()
                remote(outv.at[0], xp.at[1], in_s.at[4], in_r.at[1], {"section": later, "tower": 1 - tower}).start()

        pltpu.make_async_copy(outv.at[t], out_ref.at[t], load.at[7 + t]).start()

    for copy in started:
        copy.wait_send()

    @pl.when(first_section)
    def _():
        remote(xo.at[1], xp.at[1], in_s.at[1], in_r.at[1], other).wait_send()

    @pl.when(section < n_sec - 1)
    def _():
        remote(outv.at[0], xo.at[1], in_s.at[0], in_r.at[0], {"section": later, "tower": tower}).wait_send()
        remote(outv.at[0], xp.at[1], in_s.at[4], in_r.at[1], {"section": later, "tower": 1 - tower}).wait_send()

    for t in range(2):
        pltpu.make_async_copy(outv.at[t], out_ref.at[t], load.at[7 + t]).wait()


def shards(n_sec, n_lane, in_flight, fresh_batches, offsets, norm_gain, w_query, w_keyval, w_out):
    tok, d = in_flight.shape[2:]
    anywhere = pl.BlockSpec(memory_space=pl.ANY)
    dma = pltpu.SemaphoreType.DMA
    states = pl.pallas_call(
        functools.partial(kernel, n_sec, n_lane),
        out_shape=jax.ShapeDtypeStruct((2, tok, d), BF),
        in_specs=[anywhere, anywhere, pl.BlockSpec(memory_space=pltpu.SMEM)] + [anywhere] * 4,
        out_specs=anywhere,
        scratch_shapes=[
            pltpu.VMEM((2, tok, d), BF),
            pltpu.VMEM((2, tok, d), BF),
            pltpu.VMEM((2, 1, d), F32),
            pltpu.VMEM((d, 6 * HEAD), BF),
            pltpu.VMEM((2 * HEAD, d), BF),
            pltpu.VMEM((fresh_batches.shape[0], tok, d), BF),
            pltpu.VMEM((2, 2, 2, 8, tok, d // 2), BF),
            pltpu.VMEM((2, 8, tok, d // 2), F32),
            pltpu.VMEM((2, 2, 2, 4, tok, d // 2), BF),
            pltpu.VMEM((2, 2, 2, 4, tok, d // 2), BF),
            pltpu.VMEM((2, tok, d), BF),
            dma((2, 2, 2, 8)),
            dma((2, 2, 2, 8)),
            dma((2, 2, 2, 4)),
            dma((2, 2, 2, 4)),
            dma((5,)),
            dma((5,)),
            dma((4,)),
            dma((4,)),
            dma((9,)),
        ],
        compiler_params=pltpu.CompilerParams(collective_id=0, has_side_effects=True, vmem_limit_bytes=60 * 2**20),
        name="relay",
    )(in_flight[0, 0], fresh_batches[:, 0], offsets, norm_gain[0], w_query[0, 0], w_keyval[0, 0], w_out[0, 0])
    return states[:, None, None]


def solution(mesh):
    placed = (
        P("section", "tower", "lane", None),
        P(None, "tower", "lane", None),
        P("lane"),
        P("section", "tower", None),
        P("section", "tower", None, "lane"),
        P("section", "tower", None, None, "lane"),
        P("section", "tower", "lane", None),
    )
    return jax.shard_map(
        functools.partial(shards, mesh.shape["section"], mesh.shape["lane"]),
        mesh=mesh,
        in_specs=placed,
        out_specs=P(None, "section", "tower", "lane", None),
        check_vma=False,
    )
```

time: 285 us -> 99 us (0.35)
  the two profiles are of different devices: /device:TPU:1 before, /device:TPU:10 now
where the time goes in v1:
time: 99 us; the launch traced here: 98.8 us
  Pallas kernels  96.6 us (98%)
  local copies, waits for them, and re-layouts  1.62 us (2%)
    pallas_call x1, Pallas kernels, shards(): pl.pallas_call(functools.partial(kernel, n_sec, n_lane), out_shape=jax.Sh...  96.6 us

profile of v1, /device:TPU:10, one launch (start us, length us, event | category | flops | bytes accessed | tf_op | source)
XLA Modules:
  0.0 98.8 jit_solution(72845105366926938)
XLA Ops:
  0.7 96.6 %relay.1 = bf16[2,16,3072]{2,1,0:T(8,128)(2,1)} custom-call(bf16[16,3072]{1,0:T(8,128)(2,1)} %bitcast.14, bf16[16,16,3072]{2,1,0:T(8,128)(2,1)} %bitcast.9, s32[1]{0:T(128)S(6)} %copy.10.off_ref, f32[1,3072]{1,0:T(1,128)} %bitcast.15, bf16[3072,128]{1,0:T(8,128)(2,1)} %bitcast.12, bf16[2,3072,128]{2,1,0:T(8,128)(2,1)} %bitcast.10, bf16[128,3072]{1,0:T(8,128)(2,1)} %bitcast.13), custom_call_target="tpu_custom_call" | custom-call | tf_op jit(solution)/shard_map/relay/pallas_call | solution.py:290
  97.2 1.6 %copy.11 = bf16[2,1,1,16,3072]{4,3,2,1,0:T(8,128)(2,1)} copy(bf16[2,1,1,16,3072]{4,3,2,1,0:T(8,128)(2,1)} %bitcast.11) | data formatting | bytes 393216

commit v2 on v1

v2 whole, which is shorter than its diff:
```python
import functools
import math

import jax
import jax.numpy as jnp
from jax import lax
from jax.experimental import pallas as pl
from jax.experimental.pallas import tpu as pltpu
from jax.sharding import PartitionSpec as P

HEAD = 128
EPS = 1e-06
MESH = pl.DeviceIdType.MESH
BF = jnp.bfloat16
F32 = jnp.float32
STAGES = ((0, 1), (1, 3), (3, 5), (5, 7), (7, 8))
BACK = (0, 1, 3, 5, 7)
AHEAD = (0, 2, 4, 6, 7)
PIECES = (0, 2, 1, 3)


def normed(rows, gain):
    wide = rows.astype(F32)
    mean = jnp.mean(wide * wide, -1, keepdims=True)
    return (wide * lax.rsqrt(mean + EPS) * gain).astype(BF)


def kernel(
    n_sec,
    n_lane,
    x_ref,
    fresh_ref,
    off_ref,
    gain_ref,
    wq_ref,
    wkv_ref,
    wo_ref,
    out_ref,
    xo,
    xp,
    gains,
    w_all,
    wo_all,
    fresh,
    rows,
    part,
    rsend,
    rrecv,
    outv,
    picked,
    kv,
    off,
    ready,
    ag_s,
    ag_r,
    rs_s,
    rs_r,
    in_s,
    in_r,
    w_s,
    w_r,
    b_s,
    b_r,
    h_s,
    h_r,
    load,
):
    section = lax.axis_index("section")
    tower = lax.axis_index("tower")
    lane = lax.axis_index("lane")
    d = x_ref.shape[-1]
    hd, qd = d // 2, d // 4
    tok = x_ref.shape[0]
    up = {"lane": lax.rem(lane + 2, n_lane)}
    down = {"lane": lax.rem(lane + n_lane - 2, n_lane)}
    mate_lane = lane + 1 - 2 * lax.rem(lane, 2)
    mate = {"lane": mate_lane}
    other = {"tower": 1 - tower}
    across = {"tower": 1 - tower, "lane": mate_lane}
    later = lax.rem(section + 1, n_sec)
    sooner = lax.rem(section + n_sec - 1, n_sec)

    barrier = pltpu.get_barrier_semaphore()
    near = (up, down, mate, other)
    after = [{"section": later, "tower": t, "lane": mate_lane} for t in (tower, 1 - tower)]
    before = [{"section": sooner, "tower": t, "lane": mate_lane} for t in (tower, 1 - tower)]
    for device in near:
        pl.semaphore_signal(barrier, inc=1, device_id=device, device_id_type=MESH)

    @pl.when(section < n_sec - 1)
    def _():
        for device in after:
            pl.semaphore_signal(barrier, inc=1, device_id=device, device_id_type=MESH)

    loads = [
        (x_ref, xo.at[0]),
        (gain_ref, gains.at[0]),
        (wq_ref, w_all.at[:, pl.ds(0, HEAD)]),
        (wkv_ref.at[0], w_all.at[:, pl.ds(2 * HEAD, HEAD)]),
        (wkv_ref.at[1], w_all.at[:, pl.ds(4 * HEAD, HEAD)]),
        (wo_ref, wo_all.at[pl.ds(0, HEAD)]),
        (off_ref, off),
    ]
    loads = [pltpu.make_async_copy(a, b, load.at[i]) for i, (a, b) in enumerate(loads)]
    for copy in loads:
        copy.start()

    @pl.when(section == 0)
    def _():
        pl.semaphore_signal(barrier, inc=1, device_id=across, device_id_type=MESH)
        pl.semaphore_wait(barrier, len(near) + 1)

    @pl.when(section > 0)
    def _():
        pl.semaphore_wait(barrier, len(near) + 2)
        for device in before:
            pl.semaphore_signal(ready, inc=1, device_id=device, device_id_type=MESH)

    def remote(src, dst, send, recv, device):
        return pltpu.make_async_remote_copy(
            src_ref=src, dst_ref=dst, send_sem=send, recv_sem=recv, device_id=device, device_id_type=MESH
        )

    swaps = [
        remote(x_ref, xp.at[0], in_s.at[0], in_r.at[0], other),
        remote(gain_ref, gains.at[1], in_s.at[1], in_r.at[1], other),
        remote(wq_ref, w_all.at[:, pl.ds(HEAD, HEAD)], w_s.at[0], w_r.at[0], mate),
        remote(wkv_ref.at[0], w_all.at[:, pl.ds(3 * HEAD, HEAD)], w_s.at[1], w_r.at[1], mate),
        remote(wkv_ref.at[1], w_all.at[:, pl.ds(5 * HEAD, HEAD)], w_s.at[2], w_r.at[2], mate),
        remote(wo_ref, wo_all.at[pl.ds(HEAD, HEAD)], w_s.at[3], w_r.at[3], mate),
    ]
    for copy in swaps:
        copy.start()

    first_section = section == 0
    not_first = section > 0
    not_last = section < n_sec - 1
    pick = pltpu.make_async_copy(fresh_ref, fresh, load.at[9])

    @pl.when(first_section)
    def _():
        pick.start()

    started = list(swaps)

    def gather(t, which, half, src, dst, device):
        copy = remote(
            rows.at[t, which, half, src],
            rows.at[t, which, half, dst],
            ag_s.at[t, which, half, dst],
            ag_r.at[t, which, half, dst],
            device,
        )
        return copy

    def routes(stage, which):
        if stage < 3 or which == 0:
            yield BACK[stage], BACK[stage + 1], up
        if stage < 3 or which == 1:
            yield AHEAD[stage], AHEAD[stage + 1], down

    def pass_on(t, which, half, stage):
        for src, dst, device in routes(stage, which):
            gather(t, which, half, src, dst, device).start()

    def gathers_sent(t):
        for which in range(2):
            for half in range(2):
                for stage in range(4):
                    for src, dst, device in routes(stage, which):
                        gather(t, which, half, src, dst, device).wait_send()

    def arrive(t, which, half, slot):
        gather(t, which, half, slot, slot, up).wait_recv()

    def put_normed(t, which, raw):
        value = normed(raw, gains[which])
        for half in range(2):
            rows[t, which, half, 0] = value[:, half * hd : (half + 1) * hd]
            pass_on(t, which, half, 0)

    def partial(t, which, stage, half, first, last):
        lo, hi = STAGES[stage]
        block = rows[t, which, half, lo:hi].reshape((hi - lo) * tok, hd)
        return jnp.dot(block, w_all[half * hd : (half + 1) * hd, first:last], preferred_element_type=F32)

    def work(t, stage):
        held = {}

        def queries():
            held["q"] = (partial(t, 0, stage, 0, 0, 2 * HEAD) + partial(t, 0, stage, 1, 0, 2 * HEAD)).astype(BF)

        def keys_first():
            kv[: (STAGES[stage][1] - STAGES[stage][0]) * tok] = partial(t, 1, stage, 0, 2 * HEAD, 6 * HEAD)

        def keys_last():
            first = kv[: (STAGES[stage][1] - STAGES[stage][0]) * tok]
            held["kv"] = (first + partial(t, 1, stage, 1, 2 * HEAD, 6 * HEAD)).astype(BF)

        def mix(then=None):
            attend(stage, held["q"], held["kv"], then)

        return queries, keys_first, keys_last, mix

    def land(t, which, half, stage):
        if stage < 4:
            arrive(t, which, half, BACK[stage])
            arrive(t, which, half, AHEAD[stage])
            pass_on(t, which, half, stage)
        else:
            arrive(t, which, half, 7)

    def attend(stage, query, keyval, then=None):
        lo, hi = STAGES[stage]
        m = (hi - lo) * tok
        pieces = []
        for head in range(2):
            q = query[:, head * HEAD : (head + 1) * HEAD]
            k = keyval[:, head * HEAD : (head + 1) * HEAD]
            v = keyval[:, (2 + head) * HEAD : (3 + head) * HEAD]
            scores = lax.dot_general(q, k, (((1,), (1,)), ((), ())), preferred_element_type=F32) * (1 / math.sqrt(HEAD))
            if hi - lo > 1:
                mine = lax.broadcasted_iota(jnp.int32, (m, m), 0) // tok == lax.broadcasted_iota(jnp.int32, (m, m), 1) // tok
                scores = jnp.where(mine, scores, -jnp.inf)
            raised = jnp.exp(scores - jnp.max(scores, -1, keepdims=True))
            weights = (raised / jnp.sum(raised, -1, keepdims=True)).astype(BF)
            pieces.append(jnp.dot(weights, v, preferred_element_type=F32).astype(BF))
        mixed = jnp.concatenate(pieces, axis=1)
        for piece in PIECES:
            out = jnp.dot(mixed, wo_all[:, piece * qd : (piece + 1) * qd], preferred_element_type=F32)
            part[piece, lo:hi] = out.reshape(hi - lo, tok, qd)
            if then is not None:
                then(piece)

    def reduced(t, way, half, k):
        return remote(
            rsend.at[t, way, half, k - 1],
            rrecv.at[t, way, half, k - 1],
            rs_s.at[t, way, half, k - 1],
            rs_r.at[t, way, half, k - 1],
            down if way == 0 else up,
        )

    def reduce_step(t, way, half, k, opens):
        slot = (BACK if way == 0 else AHEAD)[k]
        value = part[half, slot]
        if not opens:
            reduced(t, way, half, k + 1).wait_recv()
            value = value + rrecv[t, way, half, k].astype(F32)
        rsend[t, way, half, k - 1] = value.astype(BF)
        copy = reduced(t, way, half, k)
        copy.start()
        started.append(copy)

    def reduce_pair(t, k, long, pieces=PIECES):
        for piece in pieces:
            way = piece // 2 if long else 1 - piece // 2
            reduce_step(t, way, piece, k, k == (4 if long else 3))

    def handed(src, piece, which, device, send):
        cols = pl.ds(piece * qd, qd)
        buffer = (xo, xp)[which]
        return remote(src.at[:, cols], buffer.at[1, :, cols], h_s.at[send, which, piece], h_r.at[which, piece], device)

    def hand_over(piece):
        return [handed(outv.at[0], piece, which, after[which], 0) for which in range(2)]

    def hand_picked(piece):
        return [handed(picked, piece, which, (mate, across)[which], 1) for which in range(2)]

    def back(piece):
        cols = pl.ds(piece * qd, qd)
        return remote(outv.at[1, :, cols], out_ref.at[1, :, cols], b_s.at[piece], b_r.at[piece], mate)

    def enter():
        for which, buffer in enumerate((xo, xp)):
            for piece in PIECES:
                handed(outv.at[0], piece, which, up, 0).wait_recv()
            put_normed(1, which, buffer[1])

    for t in range(2):
        if t == 0:
            loads[0].wait()
            loads[1].wait()
            put_normed(t, 0, xo[t])
            for half in range(2):
                land(t, 0, half, 1)
            swaps[0].wait_recv()
            swaps[1].wait_recv()
            put_normed(t, 1, xp[t])
            for copy in loads[2:]:
                copy.wait()
            for copy in swaps[2:]:
                copy.wait_recv()
            for piece in work(t, 0):
                piece()

            @pl.when(first_section)
            def _():
                pick.wait()
                picked[...] = fresh[off[0]]
                for piece in PIECES:
                    for copy in hand_picked(piece):
                        copy.start()

        else:
            pl.when(not_first)(enter)
        ahead = 1 - t
        for stage in range(1, 4):
            pieces = work(t, stage - 1) if stage > 1 or t == 1 else [None] * 4
            parts = [(0, 0, stage + ahead), (0, 1, stage + ahead), (1, 0, stage), (1, 1, stage)]
            for piece, (which, half, k) in zip(pieces, parts):
                if piece is not None:
                    piece()
                land(t, which, half, k)
        for piece in work(t, 3):
            piece()
        reduce_pair(t, 3, False)
        if t == 1:
            for half in range(2):
                land(t, 0, half, 4)
        queries, keys_first, keys_last, mix = work(t, 4)
        queries()
        land(t, 1, 0, 4)
        keys_first()
        land(t, 1, 1, 4)
        keys_last()
        mix(lambda piece: reduce_pair(t, 4, True, (piece,)))
        reduce_pair(t, 2, False)
        reduce_pair(t, 3, True)
        reduce_pair(t, 1, False)
        reduce_pair(t, 2, True)
        reduce_pair(t, 1, True)
        if t == 0:
            pl.when(first_section)(enter)
            pl.when(not_last)(lambda: pl.semaphore_wait(ready, 2))
        for piece in PIECES:
            total = part[piece, 0]
            for way in (1 - piece // 2, piece // 2):
                reduced(t, way, piece, 1).wait_recv()
                total = total + rrecv[t, way, piece, 0].astype(F32)
            cols = slice(piece * qd, (piece + 1) * qd)
            outv[t, :, cols] = (xo[t, :, cols].astype(F32) + total).astype(BF)
            if t == 1:
                back(piece).start()
            else:

                @pl.when(not_last)
                def _():
                    for copy in hand_over(piece):
                        copy.start()

        if t == 0:
            out_ref[0] = outv[0]
        else:
            gathers_sent(0)
            gathers_sent(1)

    for copy in started:
        copy.wait_send()

    @pl.when(first_section)
    def _():
        for piece in PIECES:
            for copy in hand_picked(piece):
                copy.wait_send()

    @pl.when(not_last)
    def _():
        for piece in PIECES:
            for copy in hand_over(piece):
                copy.wait_send()

    for piece in PIECES:
        back(piece).wait()


def shards(n_sec, n_lane, in_flight, fresh_batches, offsets, norm_gain, w_query, w_keyval, w_out):
    tok, d = in_flight.shape[2:]
    anywhere = pl.BlockSpec(memory_space=pl.ANY)
    dma = pltpu.SemaphoreType.DMA
    states = pl.pallas_call(
        functools.partial(kernel, n_sec, n_lane),
        out_shape=jax.ShapeDtypeStruct((2, tok, d), BF),
        in_specs=[anywhere] * 7,
        out_specs=pl.BlockSpec(memory_space=pltpu.VMEM),
        scratch_shapes=[
            pltpu.VMEM((2, tok, d), BF),
            pltpu.VMEM((2, tok, d), BF),
            pltpu.VMEM((2, 1, d), F32),
            pltpu.VMEM((d, 6 * HEAD), BF),
            pltpu.VMEM((2 * HEAD, d), BF),
            pltpu.VMEM((fresh_batches.shape[0], tok, d), BF),
            pltpu.VMEM((2, 2, 2, 8, tok, d // 2), BF),
            pltpu.VMEM((4, 8, tok, d // 4), F32),
            pltpu.VMEM((2, 2, 4, 4, tok, d // 4), BF),
            pltpu.VMEM((2, 2, 4, 4, tok, d // 4), BF),
            pltpu.VMEM((2, tok, d), BF),
            pltpu.VMEM((tok, d), BF),
            pltpu.VMEM((2 * tok, 4 * HEAD), F32),
            pltpu.SMEM((1,), jnp.int32),
            pltpu.SemaphoreType.REGULAR,
            dma((2, 2, 2, 8)),
            dma((2, 2, 2, 8)),
            dma((2, 2, 4, 4)),
            dma((2, 2, 4, 4)),
            dma((2,)),
            dma((2,)),
            dma((4,)),
            dma((4,)),
            dma((4,)),
            dma((4,)),
            dma((2, 2, 4)),
            dma((2, 4)),
            dma((10,)),
        ],
        compiler_params=pltpu.CompilerParams(collective_id=0, has_side_effects=True, vmem_limit_bytes=60 * 2**20),
        name="relay",
    )(in_flight[0, 0], fresh_batches[:, 0], offsets, norm_gain[0], w_query[0, 0], w_keyval[0, 0], w_out[0, 0])
    return states[:, None, None]


def solution(mesh):
    placed = (
        P("section", "tower", "lane", None),
        P(None, "tower", "lane", None),
        P("lane"),
        P("section", "tower", None),
        P("section", "tower", None, "lane"),
        P("section", "tower", None, None, "lane"),
        P("section", "tower", "lane", None),
    )
    return jax.shard_map(
        functools.partial(shards, mesh.shape["section"], mesh.shape["lane"]),
        mesh=mesh,
        in_specs=placed,
        out_specs=P(None, "section", "tower", "lane", None),
        check_vma=False,
    )
```

time: 99 us -> 88.1 us (0.89)
  the two profiles are of different devices: /device:TPU:10 before, /device:TPU:1 now
where the time goes in v2:
time: 88.1 us; the launch traced here: 87.8 us
  Pallas kernels  85.5 us (97%)
  local copies, waits for them, and re-layouts  1.62 us (2%)
    pallas_call x1, Pallas kernels, shards(): pl.pallas_call(functools.partial(kernel, n_sec, n_lane), out_shape=jax.Sh...  85.5 us

profile of v2, /device:TPU:1, one launch (start us, length us, event | category | flops | bytes accessed | tf_op | source)
XLA Modules:
  0.0 87.8 jit_solution(16979743837344491100)
XLA Ops:
  0.7 85.5 %relay.1 = bf16[2,16,3072]{2,1,0:T(8,128)(2,1)} custom-call(bf16[16,3072]{1,0:T(8,128)(2,1)} %bitcast.14, bf16[16,16,3072]{2,1,0:T(8,128)(2,1)} %bitcast.9, s32[1]{0:T(128)S(6)} %copy.10.off_ref, f32[1,3072]{1,0:T(1,128)} %bitcast.15, bf16[3072,128]{1,0:T(8,128)(2,1)} %bitcast.12, bf16[2,3072,128]{2,1,0:T(8,128)(2,1)} %bitcast.10, bf16[128,3072]{1,0:T(8,128)(2,1)} %bitcast.13), custom_call_target="tpu_custom_call" | custom-call | tf_op jit(solution)/shard_map/relay/pallas_call | solution.py:382
  86.1 1.6 %copy.11 = bf16[2,1,1,16,3072]{4,3,2,1,0:T(8,128)(2,1)} copy(bf16[2,1,1,16,3072]{4,3,2,1,0:T(8,128)(2,1)} %bitcast.11) | data formatting | bytes 393216

commit v3 on v2

--- a/solution.py
+++ b/solution.py
@@ -135,7 +135,7 @@
     first_section = section == 0
     not_first = section > 0
     not_last = section < n_sec - 1
-    pick = pltpu.make_async_copy(fresh_ref, fresh, load.at[9])
+    pick = pltpu.make_async_copy(fresh_ref, fresh, load.at[7])
 
     @pl.when(first_section)
     def _():
@@ -147,8 +147,8 @@
         copy = remote(
             rows.at[t, which, half, src],
             rows.at[t, which, half, dst],
-            ag_s.at[t, which, half, dst],
-            ag_r.at[t, which, half, dst],
+            ag_s.at[t],
+            ag_r.at[which, half, dst - 1],
             device,
         )
         return copy
@@ -163,12 +163,8 @@
         for src, dst, device in routes(stage, which):
             gather(t, which, half, src, dst, device).start()
 
-    def gathers_sent(t):
-        for which in range(2):
-            for half in range(2):
-                for stage in range(4):
-                    for src, dst, device in routes(stage, which):
-                        gather(t, which, half, src, dst, device).wait_send()
+    def sent(ref, sem):
+        remote(ref, ref, sem, sem, up).wait_send()
 
     def arrive(t, which, half, slot):
         gather(t, which, half, slot, slot, up).wait_recv()
@@ -204,9 +200,11 @@
 
     def land(t, which, half, stage):
         if stage < 4:
-            arrive(t, which, half, BACK[stage])
-            arrive(t, which, half, AHEAD[stage])
-            pass_on(t, which, half, stage)
+            for near_side in (BACK, AHEAD):
+                arrive(t, which, half, near_side[stage])
+                for link in routes(stage, which):
+                    if link[0] == near_side[stage]:
+                        gather(t, which, half, *link).start()
         else:
             arrive(t, which, half, 7)
 
@@ -236,8 +234,8 @@
         return remote(
             rsend.at[t, way, half, k - 1],
             rrecv.at[t, way, half, k - 1],
-            rs_s.at[t, way, half, k - 1],
-            rs_r.at[t, way, half, k - 1],
+            rs_s.at[t, k // 4],
+            rs_r.at[way, half, k - 1],
             down if way == 0 else up,
         )
 
@@ -248,9 +246,7 @@
             reduced(t, way, half, k + 1).wait_recv()
             value = value + rrecv[t, way, half, k].astype(F32)
         rsend[t, way, half, k - 1] = value.astype(BF)
-        copy = reduced(t, way, half, k)
-        copy.start()
-        started.append(copy)
+        reduced(t, way, half, k).start()
 
     def reduce_pair(t, k, long, pieces=PIECES):
         for piece in pieces:
@@ -260,7 +256,7 @@
     def handed(src, piece, which, device, send):
         cols = pl.ds(piece * qd, qd)
         buffer = (xo, xp)[which]
-        return remote(src.at[:, cols], buffer.at[1, :, cols], h_s.at[send, which, piece], h_r.at[which, piece], device)
+        return remote(src.at[:, cols], buffer.at[1, :, cols], h_s.at[send, which], h_r.at[which], device)
 
     def hand_over(piece):
         return [handed(outv.at[0], piece, which, after[which], 0) for which in range(2)]
@@ -270,12 +266,11 @@
 
     def back(piece):
         cols = pl.ds(piece * qd, qd)
-        return remote(outv.at[1, :, cols], out_ref.at[1, :, cols], b_s.at[piece], b_r.at[piece], mate)
+        return remote(outv.at[1, :, cols], out_ref.at[1, :, cols], b_s, b_r, mate)
 
     def enter():
         for which, buffer in enumerate((xo, xp)):
-            for piece in PIECES:
-                handed(outv.at[0], piece, which, up, 0).wait_recv()
+            remote(outv.at[0], buffer.at[1], h_s.at[0, which], h_r.at[which], up).wait_recv()
             put_normed(1, which, buffer[1])
 
     for t in range(2):
@@ -352,27 +347,24 @@
 
         if t == 0:
             out_ref[0] = outv[0]
-        else:
-            gathers_sent(0)
-            gathers_sent(1)
-
     for copy in started:
         copy.wait_send()
 
     @pl.when(first_section)
     def _():
-        for piece in PIECES:
-            for copy in hand_picked(piece):
-                copy.wait_send()
+        for which in range(2):
+            sent(picked, h_s.at[1, which])
 
     @pl.when(not_last)
     def _():
-        for piece in PIECES:
-            for copy in hand_over(piece):
-                copy.wait_send()
-
-    for piece in PIECES:
-        back(piece).wait()
+        for which in range(2):
+            sent(outv.at[0], h_s.at[0, which])
+
+    for t in range(2):
+        sent(rows.at[t, :, :, 0:7], ag_s.at[t])
+        sent(rsend.at[t, :, :, 0:3], rs_s.at[t, 0])
+        sent(rsend.at[t, 0, :, 3], rs_s.at[t, 1])
+    remote(outv.at[1], out_ref.at[1], b_s, b_r, mate).wait()
 
 
 def shards(n_sec, n_lane, in_flight, fresh_batches, offsets, norm_gain, w_query, w_keyval, w_out):
@@ -400,19 +392,19 @@
             pltpu.VMEM((2 * tok, 4 * HEAD), F32),
             pltpu.SMEM((1,), jnp.int32),
             pltpu.SemaphoreType.REGULAR,
-            dma((2, 2, 2, 8)),
-            dma((2, 2, 2, 8)),
-            dma((2, 2, 4, 4)),
-            dma((2, 2, 4, 4)),
+            dma((2,)),
+            dma((2, 2, 7)),
+            dma((2, 2)),
+            dma((2, 4, 4)),
             dma((2,)),
             dma((2,)),
             dma((4,)),
             dma((4,)),
-            dma((4,)),
-            dma((4,)),
-            dma((2, 2, 4)),
-            dma((2, 4)),
-            dma((10,)),
+            dma(()),
+            dma(()),
+            dma((2, 2)),
+            dma((2,)),
+            dma((8,)),
         ],
         compiler_params=pltpu.CompilerParams(collective_id=0, has_side_effects=True, vmem_limit_bytes=60 * 2**20),
         name="relay",

time: 88.1 us -> 85.6 us (0.972)
  Pallas kernels: 85.5 us -> 83.2 us
    pallas_call x1, Pallas kernels: 85.5 us -> 83.2 us  [shards(): pl.pallas_call(functools.partial(kernel, n_sec, n_lane), out_shape=jax.Sh...]
where the time goes in v3:
time: 85.6 us; the launch traced here: 85.5 us
  Pallas kernels  83.2 us (97%)
  local copies, waits for them, and re-layouts  1.62 us (2%)
    pallas_call x1, Pallas kernels, shards(): pl.pallas_call(functools.partial(kernel, n_sec, n_lane), out_shape=jax.Sh...  83.2 us

profile of v3, /device:TPU:1, one launch (start us, length us, event | category | flops | bytes accessed | tf_op | source)
XLA Modules:
  0.0 85.5 jit_solution(670120139730032383)
XLA Ops:
  0.7 83.2 %relay.1 = bf16[2,16,3072]{2,1,0:T(8,128)(2,1)} custom-call(bf16[16,3072]{1,0:T(8,128)(2,1)} %bitcast.14, bf16[16,16,3072]{2,1,0:T(8,128)(2,1)} %bitcast.9, s32[1]{0:T(128)S(6)} %copy.10.off_ref, f32[1,3072]{1,0:T(1,128)} %bitcast.15, bf16[3072,128]{1,0:T(8,128)(2,1)} %bitcast.12, bf16[2,3072,128]{2,1,0:T(8,128)(2,1)} %bitcast.10, bf16[128,3072]{1,0:T(8,128)(2,1)} %bitcast.13), custom_call_target="tpu_custom_call" | custom-call | tf_op jit(solution)/shard_map/relay/pallas_call | solution.py:374
  83.9 1.6 %copy.11 = bf16[2,1,1,16,3072]{4,3,2,1,0:T(8,128)(2,1)} copy(bf16[2,1,1,16,3072]{4,3,2,1,0:T(8,128)(2,1)} %bitcast.11) | data formatting | bytes 393216

commit v4 on v3

--- a/solution.py
+++ b/solution.py
@@ -346,7 +346,9 @@
                         copy.start()
 
         if t == 0:
-            out_ref[0] = outv[0]
+            keep = pltpu.make_async_copy(outv.at[0], out_ref.at[0], load.at[0])
+            keep.start()
+
     for copy in started:
         copy.wait_send()
 
@@ -364,6 +366,7 @@
         sent(rows.at[t, :, :, 0:7], ag_s.at[t])
         sent(rsend.at[t, :, :, 0:3], rs_s.at[t, 0])
         sent(rsend.at[t, 0, :, 3], rs_s.at[t, 1])
+    keep.wait()
     remote(outv.at[1], out_ref.at[1], b_s, b_r, mate).wait()
 
 
@@ -375,7 +378,7 @@
         functools.partial(kernel, n_sec, n_lane),
         out_shape=jax.ShapeDtypeStruct((2, tok, d), BF),
         in_specs=[anywhere] * 7,
-        out_specs=pl.BlockSpec(memory_space=pltpu.VMEM),
+        out_specs=anywhere,
         scratch_shapes=[
             pltpu.VMEM((2, tok, d), BF),
             pltpu.VMEM((2, tok, d), BF),

time: 85.6 us -> 85.1 us (level)
  no operation moved by 1% of the time
where the time goes in v4:
time: 85.1 us; the launch traced here: 84.9 us
  Pallas kernels  82.7 us (97%)
  local copies, waits for them, and re-layouts  1.62 us (2%)
    pallas_call x1, Pallas kernels, shards(): pl.pallas_call(functools.partial(kernel, n_sec, n_lane), out_shape=jax.Sh...  82.7 us

profile of v4, /device:TPU:1, one launch (start us, length us, event | category | flops | bytes accessed | tf_op | source)
XLA Modules:
  0.0 84.9 jit_solution(4391323491249598348)
XLA Ops:
  0.7 82.7 %relay.1 = bf16[2,16,3072]{2,1,0:T(8,128)(2,1)} custom-call(bf16[16,3072]{1,0:T(8,128)(2,1)} %bitcast.14, bf16[16,16,3072]{2,1,0:T(8,128)(2,1)} %bitcast.9, s32[1]{0:T(128)S(6)} %copy.10.off_ref, f32[1,3072]{1,0:T(1,128)} %bitcast.15, bf16[3072,128]{1,0:T(8,128)(2,1)} %bitcast.12, bf16[2,3072,128]{2,1,0:T(8,128)(2,1)} %bitcast.10, bf16[128,3072]{1,0:T(8,128)(2,1)} %bitcast.13), custom_call_target="tpu_custom_call" | custom-call | tf_op jit(solution)/shard_map/relay/pallas_call | solution.py:377
  83.3 1.6 %copy.11 = bf16[2,1,1,16,3072]{4,3,2,1,0:T(8,128)(2,1)} copy(bf16[2,1,1,16,3072]{4,3,2,1,0:T(8,128)(2,1)} %bitcast.11) | data formatting | bytes 393216
